TPU v7x, 32 devices: a whole 2x2x4 slice. The times are simulated.
32 devices in a mesh: groups: 2 (over y), expert: 8 (over z, core), hidden: 2 (over x), tok: 1.
Axes of the slice: x: 2, y: 2, z: 4, core: 2. Of those that a mesh axis runs over, the one named last changes fastest.
Arguments:
- out_grad: bfloat16 [2560, 1152], P(('groups', 'expert', 'tok')), parts along dimension 0, may hold values from -2.5 to 2.5
- expert_index: int32 [2560, 2], P(('groups', 'expert', 'tok')), parts along dimension 0, may hold values from 0 to 3, all different within a row; in each aligned block of 160 rows (0 to 159, 160 to 319, ...) at most 100 rows name the same one
- gate_values: float32 [2560, 2], P(('groups', 'expert', 'tok')), parts along dimension 0, may hold values from 0.2 to 1
- dispatched_inputs: bfloat16 [8, 800, 1152], P('expert', ('groups', 'tok')), parts along dimension 1, may hold values from -6 to 6
- w_gate: bfloat16 [8, 1152, 2304], P('expert', None, 'hidden'), may hold values from -0.1875 to 0.1875
- w_up: bfloat16 [8, 1152, 2304], P('expert', None, 'hidden'), may hold values from -0.1875 to 0.1875
- w_down: bfloat16 [8, 2304, 1152], P('expert', 'hidden'), may hold values from -0.09375 to 0.09375
Outputs:
- input_grad: bfloat16 [2560, 1152], P(('groups', 'expert', 'tok'), 'hidden'), parts along dimension 0
- gate_grad: bfloat16 [2560, 2], P(('groups', 'expert', 'tok')), parts along dimension 0
There are 2 independent parts, one for each index of `groups`. A program takes and returns all parts, laid end to end along the dimension named above; an argument that names none is the same for every part. Nothing has to cross between parts.
Inputs may be any that keep to these rules, and one draw needn't show every extreme that they name: `expert_index`: each row names two different experts. In each aligned block of 160 rows (the rows of one device) no expert is named by more than 100 rows, and in some block some expert is named by exactly 100 rows.
All inputs are finite; a program needn't handle non-finite values.
Results may differ from a plain program's by a relative error of at most 0.014.
Values may be sent and summed in bfloat16 or wider, within the bound.
A program may use at most 64 MiB of HBM per device.

v0:
```python
import functools
import jax
import jax.numpy as jnp
from jax import lax
from jax.experimental import pallas as pl
from jax.experimental.pallas import tpu as pltpu
from jax.sharding import PartitionSpec as P

MESH = pl.DeviceIdType.MESH
NT = (((1,), (1,)), ((), ()))


def kernel(
    pairs, capacity, start, capp, sent, saved_rows, share, lanes,
    index_hbm, values_hbm, grad_hbm, own_hbm, gate_hbm, up_hbm, down_hbm,
    out_ref, prod_ref,
    names, values, grad, places, scale_high, scale_low, send,
    w_gate, w_up, w_down, gate_pad, up_pad, saved, routed, act_a, act_b, act_c,
    part, kept, pair_out, pair_in, cross_out, cross_in, home_out, home_in,
    small_sem, weight_sem, own_sem, saved_send, saved_recv, route_send, route_recv,
    near_send, far_send, pair_send, pair_recv, cross_send, cross_recv, home_send, home_recv,
):
    index = lax.axis_index("expert")
    x = lax.axis_index("hidden")
    z = index // 2
    c = index % 2
    half = pairs // 2
    tokens, width = grad.shape
    units = w_gate.shape[1]
    rows_all = start + capp
    used = pl.ds(0, sent)
    mate = {"expert": z * 2 + (1 - c), "hidden": x}
    across = {"expert": index, "hidden": 1 - x}
    primary = x == c

    def chip(place):
        return {"expert": place * 2 + c, "hidden": x}

    def source_of(k):
        return lax.rem(z - k + pairs, pairs)

    def target_of(k):
        return lax.rem(z + k, pairs)

    def remote(src, dst, send_sem, recv_sem, device):
        return pltpu.make_async_remote_copy(
            src_ref=src, dst_ref=dst, send_sem=send_sem, recv_sem=recv_sem,
            device_id=device, device_id_type=MESH,
        )

    small = [
        pltpu.make_async_copy(index_hbm, names, small_sem.at[0]),
        pltpu.make_async_copy(grad_hbm, grad, small_sem.at[1]),
        pltpu.make_async_copy(values_hbm, values, small_sem.at[2]),
    ]
    loads = [
        pltpu.make_async_copy(gate_hbm, w_gate, weight_sem.at[0]),
        pltpu.make_async_copy(up_hbm, w_up, weight_sem.at[1]),
        pltpu.make_async_copy(down_hbm, w_down, weight_sem.at[2]),
    ]
    for which, (full, padded) in enumerate(((gate_hbm, gate_pad), (up_hbm, up_pad))):
        for h in range(2):
            loads.append(pltpu.make_async_copy(
                full.at[pl.ds(h * share, share)],
                padded.at[pl.ds(h * lanes, share)],
                weight_sem.at[3 + which * 2 + h],
            ))

    def own_part(m):
        return own_hbm.at[pl.ds(m * saved_rows, saved_rows)]

    def saved_slot(core, m):
        return saved.at[core * half + m, pl.ds(0, saved_rows)]

    own_loads = [
        pltpu.make_async_copy(own_part(m), saved_slot(c, m), own_sem.at[m]) for m in range(half)
    ]
    for load in small + own_loads + loads:
        load.start()

    barrier = pltpu.get_barrier_semaphore()
    pl.semaphore_signal(barrier, inc=1, device_id=mate, device_id_type=MESH)
    pl.semaphore_signal(barrier, inc=1, device_id=across, device_id_type=MESH)
    for k in range(1, pairs):
        pl.semaphore_signal(barrier, inc=1, device_id=chip(target_of(k)), device_id_type=MESH)

    if saved_rows < rows_all:
        saved[:, saved_rows:, :] = jnp.zeros((pairs, rows_all - saved_rows, width), jnp.bfloat16)

    if sent < capp:
        routed[:, sent:, :] = jnp.zeros((2 * pairs, capp - sent, width), jnp.bfloat16)
        home_in[:, sent:, :] = jnp.zeros((pairs, capp - sent, lanes), jnp.bfloat16)
    small[0].wait()
    experts = max(16, pairs)
    first, second = names[0:1, :], names[1:2, :]
    which_expert = lax.broadcasted_iota(jnp.int32, (experts, tokens), 0)
    member = jnp.where((which_expert == first) | (which_expert == second), 1.0, 0.0)
    earlier = jnp.where(
        lax.broadcasted_iota(jnp.int32, (tokens, tokens), 0)
        < lax.broadcasted_iota(jnp.int32, (tokens, tokens), 1), 1.0, 0.0,
    ).astype(jnp.bfloat16)
    counts = jnp.dot(member.astype(jnp.bfloat16), earlier, preferred_element_type=jnp.float32)
    places[...] = (counts + 0.5).astype(jnp.int32) + c * (capacity - start)
    row_at = lax.broadcasted_iota(jnp.int32, (capp, tokens), 0)

    def hit(e, k):
        named = names[k:k + 1, :] == e
        return (row_at == places[e:e + 1, :]) & named

    chosen = jnp.concatenate(
        [jnp.where(hit(e, 0) | hit(e, 1), 1.0, 0.0) for e in range(pairs)], axis=0
    ).astype(jnp.bfloat16)
    small[1].wait()
    send[...] = jnp.dot(chosen, grad[...], preferred_element_type=jnp.float32).astype(
        jnp.bfloat16
    ).reshape(pairs, capp, width)
    routed[index, :sent] = send[z, :sent]

    pl.semaphore_wait(barrier, pairs + 1)

    def away(k):
        place = target_of(k)
        return remote(
            send.at[place, used], routed.at[index, used], route_send.at[k], route_recv.at[index], chip(place)
        )

    @pl.when(primary)
    def _():
        for k in range(1, pairs):
            away(k).start()

    give_saved = [
        remote(own_part(m), saved_slot(c, m), saved_send.at[m], saved_recv.at[m], mate)
        for m in range(half)
    ]
    take_saved = [
        remote(own_part(m), saved_slot(1 - c, m), saved_send.at[m], saved_recv.at[m], mate)
        for m in range(half)
    ]
    for copy in give_saved:
        copy.start()
    give_route = remote(
        send.at[z, used], routed.at[index, used], route_send.at[0], route_recv.at[index], mate
    )
    give_route.start()

    small[2].wait()
    scales = jnp.concatenate(
        [
            jnp.where(hit(e, 0), values[0:1, :], jnp.where(hit(e, 1), values[1:2, :], 0.0))
            for e in range(pairs)
        ],
        axis=0,
    ).T
    high = scales.astype(jnp.bfloat16)
    scale_high[...] = high
    scale_low[...] = (scales - high.astype(jnp.float32)).astype(jnp.bfloat16)

    for h in range(2):
        for padded in (gate_pad, up_pad):
            padded[pl.ds(h * lanes + share, lanes - share), :] = jnp.zeros(
                (lanes - share, units), jnp.bfloat16
            )

    def near(k):
        block = source_of(k) * 2 + c
        return remote(
            routed.at[block, used], routed.at[block, used], near_send.at[k], route_recv.at[block], mate
        )

    def far(k):
        block = source_of(k) * 2 + c
        return remote(
            routed.at[block, used], routed.at[block, used], far_send.at[k], route_recv.at[block], across
        )

    def pass_first(k):
        @pl.when(primary)
        def _():
            near(k).wait_recv()
            far(k).start()
            near(k).start()

    def pass_second(k):
        @pl.when(jnp.logical_not(primary))
        def _():
            near(k).wait_recv()
            near(k).start()

    def wait_mate_block(k):
        block = source_of(k) * 2 + (1 - c)
        remote(
            routed.at[block, used], routed.at[block, used], near_send.at[0], route_recv.at[block], mate
        ).wait_recv()

    def forward(place):
        rows = saved[place]
        gate_pre = jnp.dot(rows, w_gate[...], preferred_element_type=jnp.float32)
        up_pre = jnp.dot(rows, w_up[...], preferred_element_type=jnp.float32)
        sig = 0.5 * jnp.tanh(0.5 * gate_pre) + 0.5
        silu = gate_pre * sig
        act_a[place] = silu
        act_b[place] = up_pre * sig * (1.0 + gate_pre * (1.0 - sig))
        act_c[place] = silu * up_pre

    def backward(k, between):
        place = source_of(k)
        low, high = routed[place * 2], routed[place * 2 + 1]
        rows = jnp.concatenate(
            [low[:start], low[start:] + high[:capp - start], high[capp - start:]], axis=0
        )
        d_hidden = lax.dot_general(rows, w_down[...], NT, preferred_element_type=jnp.float32)
        d_up = (d_hidden * act_a[place]).astype(jnp.bfloat16)
        d_gate = (d_hidden * act_b[place]).astype(jnp.bfloat16)
        product = jnp.sum(d_hidden * act_c[place], axis=1, keepdims=True)
        between()
        back = lax.dot_general(d_gate, gate_pad[...], NT, preferred_element_type=jnp.float32)
        back = back + lax.dot_general(d_up, up_pad[...], NT, preferred_element_type=jnp.float32)
        for core in range(2):
            block = slice(core * start, core * start + capp)
            for h in range(2):
                part[core, h] = back[block, h * lanes:(h + 1) * lanes]
                part[core, h, :, share:] = jnp.broadcast_to(
                    product[block], (capp, lanes - share)
                )

    def pair_copy(k):
        return remote(pair_out.at[k, :, used], pair_in.at[k, :, used], pair_send.at[k], pair_recv.at[k], mate)

    def cross_copy(k):
        return remote(cross_out.at[k, used], cross_in.at[k, used], cross_send.at[k], cross_recv.at[k], across)

    def home_copy(k):
        return remote(
            home_out.at[k, used], home_in.at[z, used], home_send.at[k], home_recv.at[z], chip(source_of(k))
        )

    def pair_start(k):
        pair_out[k] = part[1 - c].astype(jnp.bfloat16)
        pair_copy(k).start()

    def cross_start(k):
        pair_copy(k).wait_recv()
        cross_out[k] = (part[c, 1 - x] + pair_in[k, 1 - x].astype(jnp.float32)).astype(
            jnp.bfloat16
        )
        cross_copy(k).start()
        kept[k] = part[c, x] + pair_in[k, x].astype(jnp.float32)

    def reduced(k):
        cross_copy(k).wait_recv()
        return (kept[k] + cross_in[k].astype(jnp.float32)).astype(jnp.bfloat16)

    def home_start(k):
        home_out[k] = reduced(k)
        home_copy(k).start()

    for load in own_loads:
        load.wait()
    loads[0].wait()
    loads[1].wait()

    def first_phase(t, carry):
        @pl.when(t == half)
        def _():
            for copy in take_saved:
                copy.wait_recv()

        forward(lax.rem(c * half + t, pairs))

        @pl.when((t >= 1) & (t <= 2))
        def _():
            pass_first(t)

        return carry

    lax.fori_loop(0, pairs, first_phase, 0)
    for load in loads[2:]:
        load.wait()
    pass_second(1)
    if pairs > 3:
        pass_first(3)

    def second_phase(t, carry):
        k = lax.rem(t + 1, pairs)
        wait_mate_block(k)

        def between():
            @pl.when(t + 4 < pairs)
            def _():
                pass_first(t + 4)

            @pl.when(t >= 1)
            def _():
                cross_start(t)

            @pl.when(t >= 2)
            def _():
                home_start(t - 1)

        backward(k, between)
        pair_start(k)

        @pl.when(t + 2 < pairs)
        def _():
            pass_second(t + 2)

        return carry

    lax.fori_loop(0, pairs, second_phase, 0)
    cross_start(0)
    home_start(pairs - 1)
    home_in[z, :sent] = reduced(0)[:sent]

    def arrivals(k, carry):
        place = target_of(k)
        remote(
            home_out.at[k, used], home_in.at[place, used], home_send.at[k], home_recv.at[place], chip(place)
        ).wait_recv()
        return carry

    lax.fori_loop(1, pairs, arrivals, 0)

    rows = home_in[...].reshape(pairs * capp, lanes)
    total = jnp.dot(scale_high[...], rows, preferred_element_type=jnp.float32)
    total = total + jnp.dot(scale_low[...], rows, preferred_element_type=jnp.float32)
    out_ref[...] = total[:, :share].astype(jnp.bfloat16)
    for k in range(2):
        gate_row = jnp.zeros((1, tokens), jnp.float32)
        for e in range(pairs):
            column = home_in[e, :, share:share + 1].astype(jnp.float32)
            gate_row = gate_row + jnp.sum(
                jnp.where(hit(e, k), column, 0.0), axis=0, keepdims=True
            )
        prod_ref[k:k + 1, :] = gate_row.astype(jnp.bfloat16)

    for copy in give_saved:
        copy.wait_send()
    give_route.wait_send()

    def drain(k, carry):
        pair_copy(k).wait_send()
        cross_copy(k).wait_send()

        @pl.when(k > 0)
        def _():
            home_copy(k).wait_send()
            near(k).wait_send()

            @pl.when(primary)
            def _():
                away(k).wait_send()
                far(k).wait_send()

        return carry

    lax.fori_loop(0, pairs, drain, 0)


def local(out_grad, expert_index, gate_values, dispatched_inputs, w_gate, w_up, w_down):
    sources = lax.axis_size("expert")
    pairs = sources // 2
    tokens, width = out_grad.shape
    units = w_gate.shape[2]
    share = width // lax.axis_size("hidden")
    lanes = (share + 128) // 128 * 128
    capacity = 2 * dispatched_inputs.shape[1] // sources
    start = capacity // 16 * 16
    capp = (2 * capacity - start + 15) // 16 * 16
    sent = (2 * capacity - start + 7) // 8 * 8
    rows_all = start + capp
    own = dispatched_inputs[0]
    saved_rows = 2 * capacity
    if saved_rows % 8:
        own = jnp.pad(
            own.reshape(pairs // 2, saved_rows, width),
            ((0, 0), (0, rows_all - saved_rows), (0, 0)),
        ).reshape(-1, width)
        saved_rows = rows_all
    bf16, f32 = jnp.bfloat16, jnp.float32
    vmem = pl.BlockSpec(memory_space=pltpu.VMEM)
    hbm = pl.BlockSpec(memory_space=pl.ANY)
    dma = pltpu.SemaphoreType.DMA
    input_grad, gate_grad = pl.pallas_call(
        functools.partial(kernel, pairs, capacity, start, capp, sent, saved_rows, share, lanes),
        out_shape=(
            jax.ShapeDtypeStruct((tokens, share), bf16),
            jax.ShapeDtypeStruct((2, tokens), bf16),
        ),
        in_specs=[hbm] * 7,
        out_specs=(vmem, vmem),
        scratch_shapes=[
            pltpu.VMEM((2, tokens), jnp.int32),
            pltpu.VMEM((2, tokens), f32),
            pltpu.VMEM((tokens, width), bf16),
            pltpu.VMEM((max(16, pairs), tokens), jnp.int32),
            pltpu.VMEM((tokens, pairs * capp), bf16),
            pltpu.VMEM((tokens, pairs * capp), bf16),
            pltpu.VMEM((pairs, capp, width), bf16),
            pltpu.VMEM((width, units), bf16),
            pltpu.VMEM((width, units), bf16),
            pltpu.VMEM((units, width), bf16),
            pltpu.VMEM((2 * lanes, units), bf16),
            pltpu.VMEM((2 * lanes, units), bf16),
            pltpu.VMEM((pairs, rows_all, width), bf16),
            pltpu.VMEM((sources, capp, width), bf16),
            pltpu.VMEM((pairs, rows_all, units), f32),
            pltpu.VMEM((pairs, rows_all, units), f32),
            pltpu.VMEM((pairs, rows_all, units), f32),
            pltpu.VMEM((2, 2, capp, lanes), f32),
            pltpu.VMEM((pairs, capp, lanes), f32),
            pltpu.VMEM((pairs, 2, capp, lanes), bf16),
            pltpu.VMEM((pairs, 2, capp, lanes), bf16),
            pltpu.VMEM((pairs, capp, lanes), bf16),
            pltpu.VMEM((pairs, capp, lanes), bf16),
            pltpu.VMEM((pairs, capp, lanes), bf16),
            pltpu.VMEM((pairs, capp, lanes), bf16),
            dma((3,)),
            dma((7,)),
            dma((pairs // 2,)),
            dma((pairs // 2,)),
            dma((pairs // 2,)),
            dma((pairs,)),
            dma((sources,)),
            dma((pairs,)),
            dma((pairs,)),
            dma((pairs,)),
            dma((pairs,)),
            dma((pairs,)),
            dma((pairs,)),
            dma((pairs,)),
            dma((pairs,)),
        ],
        compiler_params=pltpu.CompilerParams(
            collective_id=0, has_side_effects=True, vmem_limit_bytes=60 * 1024 * 1024
        ),
    )(expert_index.T, gate_values.T, out_grad, own, w_gate[0], w_up[0], w_down[0])
    return input_grad, gate_grad.T


def solution(mesh):
    in_specs = (
        P(("groups", "expert", "tok"), None),
        P(("groups", "expert", "tok"), None),
        P(("groups", "expert", "tok"), None),
        P("expert", ("groups", "tok"), None),
        P("expert", None, "hidden"),
        P("expert", None, "hidden"),
        P("expert", "hidden", None),
    )
    out_specs = (P(("groups", "expert", "tok"), "hidden"), P(("groups", "expert", "tok"), None))
    return jax.shard_map(local, mesh=mesh, in_specs=in_specs, out_specs=out_specs, check_vma=False)
```

profile of v0, /device:TPU:0, one launch (start us, length us, event | category | flops | bytes accessed | tf_op | source)
XLA Modules:
  0.0 53.4 jit_solution(191786643726330444)
XLA Ops:
  0.6 49.9 %shard_map.86 = (bf16[160,576]{1,0:T(8,128)(2,1)}, bf16[2,160]{1,0:T(2,128)(2,1)}) custom-call(s32[2,160]{1,0:T(2,128)} %bitcast.11, f32[2,160]{1,0:T(2,128)} %bitcast.12, bf16[160,1152]{1,0:T(8,128)(2,1)} %grad_hbm.1, bf16[400,1152]{1,0:T(8,128)(2,1)} %bitcast.10, bf16[1152,1152]{1,0:T(8,128)(2,1)} %bitcast.7, bf16[1152,1152]{1,0:T(8,128)(2,1)} %bitcast.8, ...), custom_call_target="tpu_custom_call" | custom-call | tf_op jit(solution)/shard_map/pallas_call | solution.py:384
  50.6 1.6 %copy.11 = bf16[160,576]{1,0:T(8,128)(2,1)} copy(bf16[160,576]{1,0:T(8,128)(2,1)} %get-tuple-element.8) | data formatting | bytes 368640
  52.2 1.2 %copy.12 = bf16[160,2]{0,1:T(2,128)(2,1)} copy(bf16[160,2]{0,1:T(2,128)(2,1)} %bitcast.13) | data formatting | bytes 1280
where the time goes:
time: 53.6 us; the launch traced here: 53.4 us
  Pallas kernels  49.9 us (93%)
  local copies, waits for them, and re-layouts  2.82 us (5%)
  between operations  0.64 us (1%)
    pallas_call x1, Pallas kernels, local(): pl.pallas_call(functools.partial(kernel, pairs, capacity, start, capp, se...  49.9 us
    unnamed x2, local copies, waits for them, and re-layouts  2.82 us

commit v1 on v0

--- a/solution.py
+++ b/solution.py
@@ -36,11 +36,12 @@
     def chip(place):
         return {"expert": place * 2 + c, "hidden": x}
 
-    def source_of(k):
-        return lax.rem(z - k + pairs, pairs)
-
-    def target_of(k):
-        return lax.rem(z + k, pairs)
+    def partner(k):
+        place, bit = 0, 1
+        while bit < pairs:
+            place = place + lax.rem(z // bit + k // bit, 2) * bit
+            bit *= 2
+        return place
 
     def remote(src, dst, send_sem, recv_sem, device):
         return pltpu.make_async_remote_copy(
@@ -67,22 +68,22 @@
             ))
 
     def own_part(m):
-        return own_hbm.at[pl.ds(m * saved_rows, saved_rows)]
+        return own_hbm.at[pl.ds(pl.multiple_of(m * saved_rows, 8), saved_rows)]
 
     def saved_slot(core, m):
         return saved.at[core * half + m, pl.ds(0, saved_rows)]
 
-    own_loads = [
-        pltpu.make_async_copy(own_part(m), saved_slot(c, m), own_sem.at[m]) for m in range(half)
-    ]
-    for load in small + own_loads + loads:
+    def own_load(m):
+        return pltpu.make_async_copy(own_part(m), saved_slot(c, m), own_sem.at[m])
+
+    for load in small:
         load.start()
 
     barrier = pltpu.get_barrier_semaphore()
     pl.semaphore_signal(barrier, inc=1, device_id=mate, device_id_type=MESH)
     pl.semaphore_signal(barrier, inc=1, device_id=across, device_id_type=MESH)
     for k in range(1, pairs):
-        pl.semaphore_signal(barrier, inc=1, device_id=chip(target_of(k)), device_id_type=MESH)
+        pl.semaphore_signal(barrier, inc=1, device_id=chip(partner(k)), device_id_type=MESH)
 
     if saved_rows < rows_all:
         saved[:, saved_rows:, :] = jnp.zeros((pairs, rows_all - saved_rows, width), jnp.bfloat16)
@@ -91,6 +92,10 @@
         routed[:, sent:, :] = jnp.zeros((2 * pairs, capp - sent, width), jnp.bfloat16)
         home_in[:, sent:, :] = jnp.zeros((pairs, capp - sent, lanes), jnp.bfloat16)
     small[0].wait()
+    for m in range(half):
+        own_load(m).start()
+    for load in loads[:2]:
+        load.start()
     experts = max(16, pairs)
     first, second = names[0:1, :], names[1:2, :]
     which_expert = lax.broadcasted_iota(jnp.int32, (experts, tokens), 0)
@@ -116,29 +121,36 @@
     ).reshape(pairs, capp, width)
     routed[index, :sent] = send[z, :sent]
 
+    for load in loads[2:]:
+        load.start()
     pl.semaphore_wait(barrier, pairs + 1)
 
     def away(k):
-        place = target_of(k)
+        place = partner(k)
         return remote(
             send.at[place, used], routed.at[index, used], route_send.at[k], route_recv.at[index], chip(place)
         )
 
     @pl.when(primary)
     def _():
-        for k in range(1, pairs):
+        if pairs > 2:
+            away(pairs - 1).start()
+
+    away(1).start()
+
+    @pl.when(primary)
+    def _():
+        for k in range(pairs - 2, 1, -1):
             away(k).start()
 
-    give_saved = [
-        remote(own_part(m), saved_slot(c, m), saved_send.at[m], saved_recv.at[m], mate)
-        for m in range(half)
-    ]
-    take_saved = [
-        remote(own_part(m), saved_slot(1 - c, m), saved_send.at[m], saved_recv.at[m], mate)
-        for m in range(half)
-    ]
-    for copy in give_saved:
-        copy.start()
+    def give_saved(m):
+        return remote(own_part(m), saved_slot(c, m), saved_send.at[m], saved_recv.at[m], mate)
+
+    def take_saved(m):
+        return remote(own_part(m), saved_slot(1 - c, m), saved_send.at[m], saved_recv.at[m], mate)
+
+    for m in range(half):
+        give_saved(lax.rem(z + m, half)).start()
     give_route = remote(
         send.at[z, used], routed.at[index, used], route_send.at[0], route_recv.at[index], mate
     )
@@ -163,13 +175,13 @@
             )
 
     def near(k):
-        block = source_of(k) * 2 + c
+        block = partner(k) * 2 + c
         return remote(
             routed.at[block, used], routed.at[block, used], near_send.at[k], route_recv.at[block], mate
         )
 
     def far(k):
-        block = source_of(k) * 2 + c
+        block = partner(k) * 2 + c
         return remote(
             routed.at[block, used], routed.at[block, used], far_send.at[k], route_recv.at[block], across
         )
@@ -181,6 +193,10 @@
             far(k).start()
             near(k).start()
 
+    def pass_direct(k):
+        near(k).wait_recv()
+        near(k).start()
+
     def pass_second(k):
         @pl.when(jnp.logical_not(primary))
         def _():
@@ -188,7 +204,7 @@
             near(k).start()
 
     def wait_mate_block(k):
-        block = source_of(k) * 2 + (1 - c)
+        block = partner(k) * 2 + (1 - c)
         remote(
             routed.at[block, used], routed.at[block, used], near_send.at[0], route_recv.at[block], mate
         ).wait_recv()
@@ -204,7 +220,7 @@
         act_c[place] = silu * up_pre
 
     def backward(k, between):
-        place = source_of(k)
+        place = partner(k)
         low, high = routed[place * 2], routed[place * 2 + 1]
         rows = jnp.concatenate(
             [low[:start], low[start:] + high[:capp - start], high[capp - start:]], axis=0
@@ -232,7 +248,7 @@
 
     def home_copy(k):
         return remote(
-            home_out.at[k, used], home_in.at[z, used], home_send.at[k], home_recv.at[z], chip(source_of(k))
+            home_out.at[k, used], home_in.at[z, used], home_send.at[k], home_recv.at[z], chip(partner(k))
         )
 
     def pair_start(k):
@@ -255,65 +271,93 @@
         home_out[k] = reduced(k)
         home_copy(k).start()
 
-    for load in own_loads:
-        load.wait()
+    def own_home():
+        home_in[z, :sent] = reduced(0)[:sent]
+
+    def turn(t):
+        return jnp.where(t <= 1, t, pairs + 1 - t)
+
+    def ready(place):
+        m = lax.rem(place, half)
+
+        @pl.when(place // half == c)
+        def _():
+            own_load(m).wait()
+
+        @pl.when(place // half != c)
+        def _():
+            take_saved(m).wait_recv()
+
+    def nothing():
+        pass
+
     loads[0].wait()
     loads[1].wait()
-
-    def first_phase(t, carry):
-        @pl.when(t == half)
-        def _():
-            for copy in take_saved:
-                copy.wait_recv()
-
-        forward(lax.rem(c * half + t, pairs))
-
-        @pl.when((t >= 1) & (t <= 2))
-        def _():
-            pass_first(t)
-
-        return carry
-
-    lax.fori_loop(0, pairs, first_phase, 0)
+    ready(z)
+    forward(z)
     for load in loads[2:]:
         load.wait()
-    pass_second(1)
-    if pairs > 3:
-        pass_first(3)
+    wait_mate_block(0)
+    backward(0, nothing)
+    pair_start(0)
+
+    def first_phase(t, carry):
+        place = partner(turn(t))
+        ready(place)
+        forward(place)
+
+        @pl.when(t == 1)
+        def _():
+            if pairs > 2:
+                pass_first(pairs - 1)
+            cross_start(0)
+
+        @pl.when(t == min(2, pairs - 1))
+        def _():
+            pass_direct(1)
+
+        return carry
+
+    lax.fori_loop(1, pairs, first_phase, 0)
 
     def second_phase(t, carry):
-        k = lax.rem(t + 1, pairs)
+        k = turn(t)
         wait_mate_block(k)
 
         def between():
-            @pl.when(t + 4 < pairs)
+            @pl.when(t + 2 < pairs)
             def _():
-                pass_first(t + 4)
-
-            @pl.when(t >= 1)
+                pass_first(turn(t + 2))
+
+            @pl.when(t + 1 < pairs)
             def _():
-                cross_start(t)
+                pass_second(turn(t + 1))
 
             @pl.when(t >= 2)
             def _():
-                home_start(t - 1)
+                cross_start(turn(t - 1))
+
+            @pl.when(t == min(2, pairs - 1))
+            def _():
+                own_home()
+
+            @pl.when(t >= 3)
+            def _():
+                home_start(turn(t - 2))
 
         backward(k, between)
         pair_start(k)
-
-        @pl.when(t + 2 < pairs)
-        def _():
-            pass_second(t + 2)
-
         return carry
 
-    lax.fori_loop(0, pairs, second_phase, 0)
-    cross_start(0)
-    home_start(pairs - 1)
-    home_in[z, :sent] = reduced(0)[:sent]
+    lax.fori_loop(1, pairs, second_phase, 0)
+    last = turn(pairs - 1)
+    cross_start(last)
+    if pairs > 2:
+        home_start(turn(pairs - 2))
+    home_start(last)
 
     def arrivals(k, carry):
-        place = target_of(k)
+        place = partner(k)
         remote(
             home_out.at[k, used], home_in.at[place, used], home_send.at[k], home_recv.at[place], chip(place)
         ).wait_recv()
@@ -334,27 +378,27 @@
             )
         prod_ref[k:k + 1, :] = gate_row.astype(jnp.bfloat16)
 
-    for copy in give_saved:
-        copy.wait_send()
+    for m in range(half):
+        give_saved(m).wait_send()
     give_route.wait_send()
+    pair_copy(0).wait_send()
+    cross_copy(0).wait_send()
+    away(1).wait_send()
 
     def drain(k, carry):
         pair_copy(k).wait_send()
         cross_copy(k).wait_send()
-
-        @pl.when(k > 0)
-        def _():
-            home_copy(k).wait_send()
-            near(k).wait_send()
-
-            @pl.when(primary)
-            def _():
-                away(k).wait_send()
-                far(k).wait_send()
+        home_copy(k).wait_send()
+        near(k).wait_send()
+
+        @pl.when(primary & (k > 1))
+        def _():
+            away(k).wait_send()
+            far(k).wait_send()
 
         return carry
 
-    lax.fori_loop(0, pairs, drain, 0)
+    lax.fori_loop(1, pairs, drain, 0)
 
 
 def local(out_grad, expert_index, gate_values, dispatched_inputs, w_gate, w_up, w_down):

time: 53.6 us -> 50.8 us (0.948)
  Pallas kernels: 49.9 us -> 47.2 us
    pallas_call x1, Pallas kernels: 49.9 us -> 47.2 us  [local(): pl.pallas_call(functools.partial(kernel, pairs, capacity, start, capp, se...]
where the time goes in v1:
time: 50.8 us; the launch traced here: 50.6 us
  Pallas kernels  47.2 us (93%)
  local copies, waits for them, and re-layouts  2.82 us (6%)
  between operations  0.64 us (1%)
    pallas_call x1, Pallas kernels, local(): pl.pallas_call(functools.partial(kernel, pairs, capacity, start, capp, se...  47.2 us
    unnamed x2, local copies, waits for them, and re-layouts  2.82 us

profile of v1, /device:TPU:0, one launch (start us, length us, event | category | flops | bytes accessed | tf_op | source)
XLA Modules:
  0.0 50.6 jit_solution(8051126099214199571)
XLA Ops:
  0.6 47.2 %shard_map.86 = (bf16[160,576]{1,0:T(8,128)(2,1)}, bf16[2,160]{1,0:T(2,128)(2,1)}) custom-call(s32[2,160]{1,0:T(2,128)} %bitcast.11, f32[2,160]{1,0:T(2,128)} %bitcast.12, bf16[160,1152]{1,0:T(8,128)(2,1)} %grad_hbm.1, bf16[400,1152]{1,0:T(8,128)(2,1)} %bitcast.10, bf16[1152,1152]{1,0:T(8,128)(2,1)} %bitcast.7, bf16[1152,1152]{1,0:T(8,128)(2,1)} %bitcast.8, ...), custom_call_target="tpu_custom_call" | custom-call | tf_op jit(solution)/shard_map/pallas_call | solution.py:428
  47.8 1.6 %copy.11 = bf16[160,576]{1,0:T(8,128)(2,1)} copy(bf16[160,576]{1,0:T(8,128)(2,1)} %get-tuple-element.8) | data formatting | bytes 368640
  49.5 1.2 %copy.12 = bf16[160,2]{0,1:T(2,128)(2,1)} copy(bf16[160,2]{0,1:T(2,128)(2,1)} %bitcast.13) | data formatting | bytes 1280

commit v2 on v1

--- a/solution.py
+++ b/solution.py
@@ -14,7 +14,7 @@
     pairs, capacity, start, capp, sent, saved_rows, share, lanes,
     index_hbm, values_hbm, grad_hbm, own_hbm, gate_hbm, up_hbm, down_hbm,
     out_ref, prod_ref,
-    names, values, grad, places, scale_high, scale_low, send,
+    names, values, grad, places, scale, total, gate_total, send,
     w_gate, w_up, w_down, gate_pad, up_pad, saved, routed, act_a, act_b, act_c,
     part, kept, pair_out, pair_in, cross_out, cross_in, home_out, home_in,
     small_sem, weight_sem, own_sem, saved_send, saved_recv, route_send, route_recv,
@@ -133,15 +133,12 @@
 
     @pl.when(primary)
     def _():
-        if pairs > 2:
-            away(pairs - 1).start()
-
-    away(1).start()
-
-    @pl.when(primary)
+        for k in range(pairs - 1, 1, -1):
+            away(k).start()
+
+    @pl.when(jnp.logical_not(primary))
     def _():
-        for k in range(pairs - 2, 1, -1):
-            away(k).start()
+        away(1).start()
 
     def give_saved(m):
         return remote(own_part(m), saved_slot(c, m), saved_send.at[m], saved_recv.at[m], mate)
@@ -157,16 +154,11 @@
     give_route.start()
 
     small[2].wait()
-    scales = jnp.concatenate(
-        [
-            jnp.where(hit(e, 0), values[0:1, :], jnp.where(hit(e, 1), values[1:2, :], 0.0))
-            for e in range(pairs)
-        ],
-        axis=0,
-    ).T
-    high = scales.astype(jnp.bfloat16)
-    scale_high[...] = high
-    scale_low[...] = (scales - high.astype(jnp.float32)).astype(jnp.bfloat16)
+    for e in range(pairs):
+        weight = jnp.where(hit(e, 0), values[0:1, :], jnp.where(hit(e, 1), values[1:2, :], 0.0)).T
+        high = weight.astype(jnp.bfloat16)
+        scale[e, :tokens] = high
+        scale[e, tokens:] = (weight - high.astype(jnp.float32)).astype(jnp.bfloat16)
 
     for h in range(2):
         for padded in (gate_pad, up_pad):
@@ -218,6 +210,9 @@
         act_a[place] = silu
         act_b[place] = up_pre * sig * (1.0 + gate_pre * (1.0 - sig))
         act_c[place] = silu * up_pre
+
+    def slot(k):
+        return 1 if isinstance(k, int) and k == 0 else 0
 
     def backward(k, between):
         place = partner(k)
@@ -235,8 +230,8 @@
         for core in range(2):
             block = slice(core * start, core * start + capp)
             for h in range(2):
-                part[core, h] = back[block, h * lanes:(h + 1) * lanes]
-                part[core, h, :, share:] = jnp.broadcast_to(
+                part[slot(k), core, h] = back[block, h * lanes:(h + 1) * lanes]
+                part[slot(k), core, h, :, share:] = jnp.broadcast_to(
                     product[block], (capp, lanes - share)
                 )
 
@@ -252,16 +247,16 @@
         )
 
     def pair_start(k):
-        pair_out[k] = part[1 - c].astype(jnp.bfloat16)
+        pair_out[k] = part[slot(k), 1 - c].astype(jnp.bfloat16)
         pair_copy(k).start()
 
     def cross_start(k):
         pair_copy(k).wait_recv()
-        cross_out[k] = (part[c, 1 - x] + pair_in[k, 1 - x].astype(jnp.float32)).astype(
+        cross_out[k] = (part[slot(k), c, 1 - x] + pair_in[k, 1 - x].astype(jnp.float32)).astype(
             jnp.bfloat16
         )
         cross_copy(k).start()
-        kept[k] = part[c, x] + pair_in[k, x].astype(jnp.float32)
+        kept[k] = part[slot(k), c, x] + pair_in[k, x].astype(jnp.float32)
 
     def reduced(k):
         cross_copy(k).wait_recv()
@@ -275,7 +270,14 @@
         home_in[z, :sent] = reduced(0)[:sent]
 
     def turn(t):
-        return jnp.where(t <= 1, t, pairs + 1 - t)
+        return pairs - t
+
+    def steps(body):
+        if pairs <= 4:
+            for t in range(1, pairs):
+                body(t, 0)
+        else:
+            lax.fori_loop(1, pairs, body, 0)
 
     def ready(place):
         m = lax.rem(place, half)
@@ -301,6 +303,12 @@
     backward(0, nothing)
     pair_start(0)
 
+    @pl.when(primary)
+    def _():
+        away(1).start()
+
+    relayed = pairs > 2
+
     def first_phase(t, carry):
         place = partner(turn(t))
         ready(place)
@@ -308,75 +316,98 @@
 
         @pl.when(t == 1)
         def _():
-            if pairs > 2:
+            if relayed:
                 pass_first(pairs - 1)
-            cross_start(0)
-
-        @pl.when(t == min(2, pairs - 1))
+
+        return carry
+
+    steps(first_phase)
+
+    if relayed:
+        @pl.when(jnp.logical_not(primary))
         def _():
             pass_direct(1)
 
-        return carry
-
-    lax.fori_loop(1, pairs, first_phase, 0)
+        pass_second(pairs - 1)
+        pass_first(pairs - 2)
+    else:
+        pass_direct(1)
 
     def second_phase(t, carry):
         k = turn(t)
         wait_mate_block(k)
 
-        def between():
-            @pl.when(t + 2 < pairs)
+        backward(k, nothing)
+        pair_start(k)
+
+        @pl.when(t + 2 < pairs)
+        def _():
+            pass_second(turn(t + 1))
+
+        @pl.when(t + 3 < pairs)
+        def _():
+            pass_first(turn(t + 2))
+
+        @pl.when((t >= 2) & (t + 1 < pairs))
+        def _():
+            home_start(turn(t - 1))
+
+        cross_start(k)
+
+        @pl.when(t == 1)
+        def _():
+            cross_start(0)
+
+            @pl.when(primary & relayed)
             def _():
-                pass_first(turn(t + 2))
-
-            @pl.when(t + 1 < pairs)
-            def _():
-                pass_second(turn(t + 1))
-
-            @pl.when(t >= 2)
-            def _():
-                cross_start(turn(t - 1))
-
-            @pl.when(t == min(2, pairs - 1))
-            def _():
-                own_home()
-
-            @pl.when(t >= 3)
-            def _():
-                home_start(turn(t - 2))
-
-        backward(k, between)
-        pair_start(k)
+                pass_direct(1)
+
         return carry
 
-    lax.fori_loop(1, pairs, second_phase, 0)
-    last = turn(pairs - 1)
-    cross_start(last)
-    if pairs > 2:
-        home_start(turn(pairs - 2))
-    home_start(last)
-
-    def arrivals(k, carry):
+    steps(second_phase)
+    own_home()
+    if relayed:
+        home_start(2)
+    home_start(1)
+
+    def gather(place, first):
+        rows = home_in[place]
+        sums = jnp.dot(scale[place], rows, preferred_element_type=jnp.float32)
+        column = rows[:, share:share + 1].astype(jnp.float32)
+        gates = jnp.concatenate(
+            [
+                jnp.sum(
+                    jnp.where(
+                        (row_at == places[pl.ds(place, 1), :]) & (names[k:k + 1, :] == place), column, 0.0
+                    ),
+                    axis=0, keepdims=True,
+                )
+                for k in range(2)
+            ],
+            axis=0,
+        )
+        sums = sums[:tokens] + sums[tokens:]
+        return (sums, gates) if first else (total[...] + sums, gate_total[...] + gates)
+
+    total[...], gate_total[...] = gather(z, True)
+
+    def arrived(k):
         place = partner(k)
         remote(
             home_out.at[k, used], home_in.at[place, used], home_send.at[k], home_recv.at[place], chip(place)
         ).wait_recv()
+        return place
+
+    def add(t, carry):
+        total[...], gate_total[...] = gather(arrived(pairs + 1 - t), False)
         return carry
 
-    lax.fori_loop(1, pairs, arrivals, 0)
-
-    rows = home_in[...].reshape(pairs * capp, lanes)
-    total = jnp.dot(scale_high[...], rows, preferred_element_type=jnp.float32)
-    total = total + jnp.dot(scale_low[...], rows, preferred_element_type=jnp.float32)
-    out_ref[...] = total[:, :share].astype(jnp.bfloat16)
-    for k in range(2):
-        gate_row = jnp.zeros((1, tokens), jnp.float32)
-        for e in range(pairs):
-            column = home_in[e, :, share:share + 1].astype(jnp.float32)
-            gate_row = gate_row + jnp.sum(
-                jnp.where(hit(e, k), column, 0.0), axis=0, keepdims=True
-            )
-        prod_ref[k:k + 1, :] = gate_row.astype(jnp.bfloat16)
+    lax.fori_loop(2, pairs - 1, add, 0)
+    if relayed:
+        total[...], gate_total[...] = gather(arrived(1), False)
+    sums, gates = gather(arrived(2 if relayed else 1), False)
+    out_ref[...] = sums[:, :share].astype(jnp.bfloat16)
+    prod_ref[...] = gates.astype(jnp.bfloat16)
 
     for m in range(half):
         give_saved(m).wait_send()
@@ -428,8 +459,8 @@
     input_grad, gate_grad = pl.pallas_call(
         functools.partial(kernel, pairs, capacity, start, capp, sent, saved_rows, share, lanes),
         out_shape=(
-            jax.ShapeDtypeStruct((tokens, share), bf16),
-            jax.ShapeDtypeStruct((2, tokens), bf16),
+            pltpu.VMEM((tokens, share), bf16),
+            pltpu.VMEM((2, tokens), bf16),
         ),
         in_specs=[hbm] * 7,
         out_specs=(vmem, vmem),
@@ -438,8 +469,9 @@
             pltpu.VMEM((2, tokens), f32),
             pltpu.VMEM((tokens, width), bf16),
             pltpu.VMEM((max(16, pairs), tokens), jnp.int32),
-            pltpu.VMEM((tokens, pairs * capp), bf16),
-            pltpu.VMEM((tokens, pairs * capp), bf16),
+            pltpu.VMEM((pairs, 2 * tokens, capp), bf16),
+            pltpu.VMEM((tokens, lanes), f32),
+            pltpu.VMEM((2, tokens), f32),
             pltpu.VMEM((pairs, capp, width), bf16),
             pltpu.VMEM((width, units), bf16),
             pltpu.VMEM((width, units), bf16),
@@ -451,7 +483,7 @@
             pltpu.VMEM((pairs, rows_all, units), f32),
             pltpu.VMEM((pairs, rows_all, units), f32),
             pltpu.VMEM((pairs, rows_all, units), f32),
-            pltpu.VMEM((2, 2, capp, lanes), f32),
+            pltpu.VMEM((2, 2, 2, capp, lanes), f32),
             pltpu.VMEM((pairs, capp, lanes), f32),
             pltpu.VMEM((pairs, 2, capp, lanes), bf16),
             pltpu.VMEM((pairs, 2, capp, lanes), bf16),

time: 50.8 us -> 47.3 us (0.931)
  Pallas kernels: 47.2 us -> 45.2 us
  local copies, waits for them, and re-layouts: 2.82 us -> 1.24 us
    pallas_call x1, Pallas kernels: 47.2 us -> 45.2 us  [local(): pl.pallas_call(functools.partial(kernel, pairs, capacity, start, capp, se...]
    unnamed x2, local copies, waits for them, and re-layouts: 2.82 us -> 1.24 us
where the time goes in v2:
time: 47.3 us; the launch traced here: 47.1 us
  Pallas kernels  45.2 us (96%)
  local copies, waits for them, and re-layouts  1.24 us (3%)
  between operations  0.64 us (1%)
    pallas_call x1, Pallas kernels, local(): pl.pallas_call(functools.partial(kernel, pairs, capacity, start, capp, se...  45.2 us
    unnamed x2, local copies, waits for them, and re-layouts  1.24 us

profile of v2, /device:TPU:0, one launch (start us, length us, event | category | flops | bytes accessed | tf_op | source)
XLA Modules:
  0.0 47.1 jit_solution(15697328848691788845)
XLA Ops:
  0.6 45.2 %shard_map.86 = (bf16[160,576]{1,0:T(8,128)(2,1)S(1)}, bf16[2,160]{1,0:T(2,128)(2,1)S(1)}) custom-call(s32[2,160]{1,0:T(2,128)} %bitcast.12, f32[2,160]{1,0:T(2,128)} %bitcast.13, bf16[160,1152]{1,0:T(8,128)(2,1)} %grad_hbm.1, bf16[400,1152]{1,0:T(8,128)(2,1)} %bitcast.11, bf16[1152,1152]{1,0:T(8,128)(2,1)} %bitcast.8, bf16[1152,1152]{1,0:T(8,128)(2,1)} %bitcast.9, ...), custom_call_target="tpu_custom_call" | custom-call | tf_op jit(solution)/shard_map/pallas_call | solution.py:459
  45.9 0.7 %copy.11 = bf16[160,576]{1,0:T(8,128)(2,1)} copy(bf16[160,576]{1,0:T(8,128)(2,1)S(1)} %get-tuple-element.6) | data formatting | bytes 368640
  46.6 0.6 %copy.12 = bf16[160,2]{0,1:T(2,128)(2,1)} copy(bf16[160,2]{0,1:T(2,128)(2,1)S(1)} %bitcast.7) | data formatting | bytes 1280

commit v3 on v2

--- a/solution.py
+++ b/solution.py
@@ -29,6 +29,9 @@
     units = w_gate.shape[1]
     rows_all = start + capp
     used = pl.ds(0, sent)
+    slabs = share // 128
+    fold = pair_out.shape[2] - slabs * sent - 8
+    tail = slabs * sent + fold
     mate = {"expert": z * 2 + (1 - c), "hidden": x}
     across = {"expert": index, "hidden": 1 - x}
     primary = x == c
@@ -90,7 +93,6 @@
 
     if sent < capp:
         routed[:, sent:, :] = jnp.zeros((2 * pairs, capp - sent, width), jnp.bfloat16)
-        home_in[:, sent:, :] = jnp.zeros((pairs, capp - sent, lanes), jnp.bfloat16)
     small[0].wait()
     for m in range(half):
         own_load(m).start()
@@ -155,7 +157,7 @@
 
     small[2].wait()
     for e in range(pairs):
-        weight = jnp.where(hit(e, 0), values[0:1, :], jnp.where(hit(e, 1), values[1:2, :], 0.0)).T
+        weight = jnp.where(hit(e, 0), values[0:1, :], jnp.where(hit(e, 1), values[1:2, :], 0.0))[:sent].T
         high = weight.astype(jnp.bfloat16)
         scale[e, :tokens] = high
         scale[e, tokens:] = (weight - high.astype(jnp.float32)).astype(jnp.bfloat16)
@@ -227,23 +229,32 @@
         between()
         back = lax.dot_general(d_gate, gate_pad[...], NT, preferred_element_type=jnp.float32)
         back = back + lax.dot_general(d_up, up_pad[...], NT, preferred_element_type=jnp.float32)
+        diagonal = lax.broadcasted_iota(jnp.int32, (sent, 128), 0) == lax.broadcasted_iota(
+            jnp.int32, (sent, 128), 1
+        )
         for core in range(2):
-            block = slice(core * start, core * start + capp)
+            block = slice(core * start, core * start + sent)
+            gates = jnp.sum(jnp.where(diagonal, product[block], 0.0), axis=0, keepdims=True)
             for h in range(2):
-                part[slot(k), core, h] = back[block, h * lanes:(h + 1) * lanes]
-                part[slot(k), core, h, :, share:] = jnp.broadcast_to(
-                    product[block], (capp, lanes - share)
-                )
+                half_back = back[block, h * lanes:(h + 1) * lanes]
+                for j in range(slabs):
+                    part[slot(k), core, h, j * sent:(j + 1) * sent] = half_back[:, j * 128:(j + 1) * 128]
+                if fold:
+                    rest = half_back[:, slabs * 128:]
+                    if fold < sent:
+                        rest = rest[:fold] + pltpu.roll(rest[sent - fold:], 64, 1)
+                    part[slot(k), core, h, slabs * sent:tail] = rest
+                part[slot(k), core, h, tail:] = jnp.broadcast_to(gates, (8, 128))
 
     def pair_copy(k):
-        return remote(pair_out.at[k, :, used], pair_in.at[k, :, used], pair_send.at[k], pair_recv.at[k], mate)
+        return remote(pair_out.at[k], pair_in.at[k], pair_send.at[k], pair_recv.at[k], mate)
 
     def cross_copy(k):
-        return remote(cross_out.at[k, used], cross_in.at[k, used], cross_send.at[k], cross_recv.at[k], across)
+        return remote(cross_out.at[k], cross_in.at[k], cross_send.at[k], cross_recv.at[k], across)
 
     def home_copy(k):
         return remote(
-            home_out.at[k, used], home_in.at[z, used], home_send.at[k], home_recv.at[z], chip(partner(k))
+            home_out.at[k], home_in.at[z], home_send.at[k], home_recv.at[z], chip(partner(k))
         )
 
     def pair_start(k):
@@ -267,7 +278,7 @@
         home_copy(k).start()
 
     def own_home():
-        home_in[z, :sent] = reduced(0)[:sent]
+        home_in[z] = reduced(0)
 
     def turn(t):
         return pairs - t
@@ -371,17 +382,25 @@
     home_start(1)
 
     def gather(place, first):
-        rows = home_in[place]
-        sums = jnp.dot(scale[place], rows, preferred_element_type=jnp.float32)
-        column = rows[:, share:share + 1].astype(jnp.float32)
+        packed = home_in[place]
+        columns = [packed[j * sent:(j + 1) * sent] for j in range(slabs)]
+        if fold:
+            rest = packed[slabs * sent:tail]
+            if fold < sent:
+                rest = rest.astype(jnp.float32)
+                lower = pltpu.roll(rest, 64, 1)[2 * fold - sent:]
+                rest = jnp.concatenate([rest, lower], axis=0).astype(jnp.bfloat16)
+            columns.append(rest)
+        sums = jnp.dot(scale[place], jnp.concatenate(columns, axis=1), preferred_element_type=jnp.float32)
+        product = packed[tail:, :sent]
+        taken = row_at[:sent] == places[pl.ds(place, 1), :]
         gates = jnp.concatenate(
             [
-                jnp.sum(
-                    jnp.where(
-                        (row_at == places[pl.ds(place, 1), :]) & (names[k:k + 1, :] == place), column, 0.0
-                    ),
-                    axis=0, keepdims=True,
-                )
+                jnp.dot(
+                    product,
+                    jnp.where(taken & (names[k:k + 1, :] == place), 1.0, 0.0).astype(jnp.bfloat16),
+                    preferred_element_type=jnp.float32,
+                )[:1]
                 for k in range(2)
             ],
             axis=0,
@@ -394,7 +413,7 @@
     def arrived(k):
         place = partner(k)
         remote(
-            home_out.at[k, used], home_in.at[place, used], home_send.at[k], home_recv.at[place], chip(place)
+            home_out.at[k], home_in.at[place], home_send.at[k], home_recv.at[place], chip(place)
         ).wait_recv()
         return place
 
@@ -444,6 +463,10 @@
     capp = (2 * capacity - start + 15) // 16 * 16
     sent = (2 * capacity - start + 7) // 8 * 8
     rows_all = start + capp
+    assert sent <= 128
+    fold = 0 if share % 128 == 0 else (sent + 15) // 16 * 8 if share % 128 == 64 else sent
+    packed = share // 128 * sent + fold + 8
+    wide = (share + 127) // 128 * 128
     own = dispatched_inputs[0]
     saved_rows = 2 * capacity
     if saved_rows % 8:
@@ -469,8 +492,8 @@
             pltpu.VMEM((2, tokens), f32),
             pltpu.VMEM((tokens, width), bf16),
             pltpu.VMEM((max(16, pairs), tokens), jnp.int32),
-            pltpu.VMEM((pairs, 2 * tokens, capp), bf16),
-            pltpu.VMEM((tokens, lanes), f32),
+            pltpu.VMEM((pairs, 2 * tokens, sent), bf16),
+            pltpu.VMEM((tokens, wide), f32),
             pltpu.VMEM((2, tokens), f32),
             pltpu.VMEM((pairs, capp, width), bf16),
             pltpu.VMEM((width, units), bf16),
@@ -483,14 +506,14 @@
             pltpu.VMEM((pairs, rows_all, units), f32),
             pltpu.VMEM((pairs, rows_all, units), f32),
             pltpu.VMEM((pairs, rows_all, units), f32),
-            pltpu.VMEM((2, 2, 2, capp, lanes), f32),
-            pltpu.VMEM((pairs, capp, lanes), f32),
-            pltpu.VMEM((pairs, 2, capp, lanes), bf16),
-            pltpu.VMEM((pairs, 2, capp, lanes), bf16),
-            pltpu.VMEM((pairs, capp, lanes), bf16),
-            pltpu.VMEM((pairs, capp, lanes), bf16),
-            pltpu.VMEM((pairs, capp, lanes), bf16),
-            pltpu.VMEM((pairs, capp, lanes), bf16),
+            pltpu.VMEM((2, 2, 2, packed, 128), f32),
+            pltpu.VMEM((pairs, packed, 128), f32),
+            pltpu.VMEM((pairs, 2, packed, 128), bf16),
+            pltpu.VMEM((pairs, 2, packed, 128), bf16),
+            pltpu.VMEM((pairs, packed, 128), bf16),
+            pltpu.VMEM((pairs, packed, 128), bf16),
+            pltpu.VMEM((pairs, packed, 128), bf16),
+            pltpu.VMEM((pairs, packed, 128), bf16),
             dma((3,)),
             dma((7,)),
             dma((pairs // 2,)),

time: 47.3 us -> 46.6 us (0.985)
  Pallas kernels: 45.2 us -> 44.5 us
    pallas_call x1, Pallas kernels: 45.2 us -> 44.5 us  [local(): pl.pallas_call(functools.partial(kernel, pairs, capacity, start, capp, se...]
where the time goes in v3:
time: 46.6 us; the launch traced here: 46.4 us
  Pallas kernels  44.5 us (95%)
  local copies, waits for them, and re-layouts  1.24 us (3%)
  between operations  0.64 us (1%)
    pallas_call x1, Pallas kernels, local(): pl.pallas_call(functools.partial(kernel, pairs, capacity, start, capp, se...  44.5 us
    unnamed x2, local copies, waits for them, and re-layouts  1.24 us

profile of v3, /device:TPU:0, one launch (start us, length us, event | category | flops | bytes accessed | tf_op | source)
XLA Modules:
  0.0 46.4 jit_solution(16419533294164169988)
XLA Ops:
  0.6 44.5 %shard_map.86 = (bf16[160,576]{1,0:T(8,128)(2,1)S(1)}, bf16[2,160]{1,0:T(2,128)(2,1)S(1)}) custom-call(s32[2,160]{1,0:T(2,128)} %bitcast.12, f32[2,160]{1,0:T(2,128)} %bitcast.13, bf16[160,1152]{1,0:T(8,128)(2,1)} %grad_hbm.1, bf16[400,1152]{1,0:T(8,128)(2,1)} %bitcast.11, bf16[1152,1152]{1,0:T(8,128)(2,1)} %bitcast.8, bf16[1152,1152]{1,0:T(8,128)(2,1)} %bitcast.9, ...), custom_call_target="tpu_custom_call" | custom-call | tf_op jit(solution)/shard_map/pallas_call | solution.py:482
  45.2 0.7 %copy.11 = bf16[160,576]{1,0:T(8,128)(2,1)} copy(bf16[160,576]{1,0:T(8,128)(2,1)S(1)} %get-tuple-element.6) | data formatting | bytes 368640
  45.9 0.6 %copy.12 = bf16[160,2]{0,1:T(2,128)(2,1)} copy(bf16[160,2]{0,1:T(2,128)(2,1)S(1)} %bitcast.7) | data formatting | bytes 1280

commit v4 on v3

--- a/solution.py
+++ b/solution.py
@@ -359,11 +359,11 @@
         def _():
             pass_first(turn(t + 2))
 
+        cross_start(k)
+
         @pl.when((t >= 2) & (t + 1 < pairs))
         def _():
             home_start(turn(t - 1))
-
-        cross_start(k)
 
         @pl.when(t == 1)
         def _():

time: 46.6 us -> 46.7 us (level)
  no operation moved by 1% of the time
where the time goes in v4:
time: 46.7 us; the launch traced here: 46.5 us
  Pallas kernels  44.6 us (96%)
  local copies, waits for them, and re-layouts  1.24 us (3%)
  between operations  0.64 us (1%)
    pallas_call x1, Pallas kernels, local(): pl.pallas_call(functools.partial(kernel, pairs, capacity, start, capp, se...  44.6 us
    unnamed x2, local copies, waits for them, and re-layouts  1.24 us

profile of v4, /device:TPU:0, one launch (start us, length us, event | category | flops | bytes accessed | tf_op | source)
XLA Modules:
  0.0 46.5 jit_solution(6786155457450223504)
XLA Ops:
  0.6 44.6 %shard_map.86 = (bf16[160,576]{1,0:T(8,128)(2,1)S(1)}, bf16[2,160]{1,0:T(2,128)(2,1)S(1)}) custom-call(s32[2,160]{1,0:T(2,128)} %bitcast.12, f32[2,160]{1,0:T(2,128)} %bitcast.13, bf16[160,1152]{1,0:T(8,128)(2,1)} %grad_hbm.1, bf16[400,1152]{1,0:T(8,128)(2,1)} %bitcast.11, bf16[1152,1152]{1,0:T(8,128)(2,1)} %bitcast.8, bf16[1152,1152]{1,0:T(8,128)(2,1)} %bitcast.9, ...), custom_call_target="tpu_custom_call" | custom-call | tf_op jit(solution)/shard_map/pallas_call | solution.py:482
  45.3 0.7 %copy.11 = bf16[160,576]{1,0:T(8,128)(2,1)} copy(bf16[160,576]{1,0:T(8,128)(2,1)S(1)} %get-tuple-element.6) | data formatting | bytes 368640
  45.9 0.6 %copy.12 = bf16[160,2]{0,1:T(2,128)(2,1)} copy(bf16[160,2]{0,1:T(2,128)(2,1)S(1)} %bitcast.7) | data formatting | bytes 1280
